TPU v7x, 256 devices: a whole 4x4x8 slice. The times are simulated.
256 devices in a mesh: seq: 32 (over z, x), head: 8 (over y, core).
Axes of the slice: x: 4, y: 4, z: 8, core: 2. Of those that a mesh axis runs over, the one named last changes fastest.
Arguments:
- queries: bfloat16 [32768, 8192], P('seq', 'head'), may hold values from -6 to 6
- key_vectors: bfloat16 [32768, 8192], P('seq', 'head'), may hold values from -6 to 6
- value_vectors: bfloat16 [32768, 8192], P('seq', 'head'), may hold values from -6 to 6
- level_weight: float32 [32768, 1024], P('seq', 'head'), may hold values from 0.02 to 1
- gate_values: bfloat16 [32768, 8192], P(('seq', 'head')), may hold values from -6 to 6
- norm_gain: float32 [8192], replicated, may hold values from 0.5 to 1.5
Outputs:
- normed: bfloat16 [32768, 8192], P(('seq', 'head'))
All inputs are finite; a program needn't handle non-finite values.
Results may differ from a plain program's by a relative error of at most 0.012.
Values may be sent and summed in bfloat16 or wider, within the bound.
A program may use at most 128 MiB of HBM per device.

v0:
```python
import jax
import jax.numpy as jnp
from jax import lax
from jax.sharding import PartitionSpec as P

HEAD_DIM = 128
LEVELS = 16


def swapped(array, axis, bit):
    return lax.ppermute(array, axis, [(i, i ^ 1 << bit) for i in range(lax.axis_size(axis))])


def bit_levels(count):
    indices = jnp.arange(count, dtype=jnp.int32)
    mixed = jnp.bitwise_xor(indices[:, None], indices[None, :])
    levels = jnp.zeros((count, count), jnp.int32)
    for height in range(count.bit_length() - 1):
        levels = levels + (mixed >= 1 << height).astype(jnp.int32)
    causal = indices[None, :] <= indices[:, None]
    return (levels, causal)


def local_attention(query_head, key_head, value_head, weight_head, levels, causal):
    scores = jnp.dot(query_head, key_head.T, preferred_element_type=jnp.float32)
    factor = jnp.zeros(scores.shape, jnp.float32)
    for height in range(query_head.shape[0].bit_length()):
        factor = factor + jnp.where(
            levels == height, weight_head[:, height : height + 1], jnp.float32(0.0)
        )
    weighted = jnp.where(causal, scores * factor, jnp.float32(0.0)).astype(jnp.bfloat16)
    return jnp.dot(weighted, value_head, preferred_element_type=jnp.float32)


def per_device(queries, key_vectors, value_vectors, level_weight, gate_values, norm_gain):
    count, features = queries.shape
    heads_here = features // HEAD_DIM
    query_rows = queries.reshape(count, heads_here, HEAD_DIM)
    key_rows = key_vectors.reshape(count, heads_here, HEAD_DIM)
    value_rows = value_vectors.reshape(count, heads_here, HEAD_DIM)
    weight_rows = level_weight.reshape(count, heads_here, LEVELS)
    states = jnp.einsum("che,chf->hef", key_rows, value_rows, preferred_element_type=jnp.float32)
    position = lax.axis_index("seq")
    seq_bits = lax.axis_size("seq").bit_length() - 1
    local_bits = count.bit_length() - 1
    running = states
    collected = []
    for height in range(seq_bits):
        partner = swapped(running.astype(jnp.bfloat16), "seq", height).astype(running.dtype)
        upper = (jnp.right_shift(position, height) & 1).astype(jnp.float32)
        collected.append(partner * upper)
        running = running + partner
    level_sums = jnp.stack(collected)
    rounded = level_sums.astype(jnp.bfloat16)
    cross = jnp.zeros((count, heads_here, HEAD_DIM), jnp.float32)
    for height in range(seq_bits):
        term = jnp.einsum(
            "che,hef->chf", query_rows, rounded[height], preferred_element_type=jnp.float32
        )
        cross = cross + weight_rows[:, :, local_bits + 1 + height, None] * term
    levels, causal = bit_levels(count)

    def per_head(head_inputs):
        return local_attention(
            head_inputs[0], head_inputs[1], head_inputs[2], head_inputs[3], levels, causal
        )

    inner = lax.map(
        per_head,
        (
            query_rows.transpose(1, 0, 2),
            key_rows.transpose(1, 0, 2),
            value_rows.transpose(1, 0, 2),
            weight_rows.transpose(1, 0, 2),
        ),
    )
    inner = inner.transpose(1, 0, 2)
    attended = (inner + cross).reshape(count, features).astype(jnp.bfloat16)
    token_rows = lax.all_to_all(attended, "head", split_axis=0, concat_axis=1, tiled=True).astype(
        jnp.float32
    )
    mean_square = jnp.mean(token_rows * token_rows, axis=1, keepdims=True)
    gating = jax.nn.silu(gate_values.astype(jnp.float32))
    return (token_rows * lax.rsqrt(mean_square + 1e-06) * norm_gain[None, :] * gating).astype(
        jnp.bfloat16
    )


def solution(mesh):
    placed = (
        P("seq", "head"),
        P("seq", "head"),
        P("seq", "head"),
        P("seq", "head"),
        P(("seq", "head"), None),
        P(),
    )
    return jax.shard_map(
        per_device, mesh=mesh, in_specs=placed, out_specs=P(("seq", "head"), None), check_vma=False
    )
```

profile of v0, /device:TPU:1, one launch (start us, length us, event | category | flops | bytes accessed | tf_op | source)
XLA Modules:
  0.0 152.5 jit_solution(2829906529884983937)
XLA Ops:
  0.0 2.9 %copy.37 = bf16[1024,1024]{0,1:T(8,128)(2,1)S(1)} copy(bf16[1024,1024]{1,0:T(8,128)(2,1)} %param.9) | data formatting | bytes 4194304 | tf_op args[1]
  2.9 4.6 %copy.39 = bf16[1024,1024]{0,1:T(8,128)(2,1)} copy(bf16[1024,1024]{1,0:T(8,128)(2,1)} %param.10) | data formatting | bytes 4194304 | tf_op args[2]
  7.5 3.0 %fusion.80 = (bf16[8,128,128]{2,1,0:T(8,128)(2,1)}, f32[8,128,128]{2,1,0:T(8,128)S(1)}) fusion(bf16[1024,8,128]{0,2,1:T(8,128)(2,1)S(1)} %bitcast.141, bf16[1024,8,128]{0,2,1:T(8,128)(2,1)} %bitcast.143), kind=kOutput, calls=%fused_computation.97 | convolution fusion | flops 268566528 | bytes 4980736 | tf_op jit(solution)/shard_map/che,chf->hef/dot_general | solution.py:42
  12.5 2.9 %copy.36 = bf16[1024,1024]{0,1:T(8,128)(2,1)S(1)} copy(bf16[1024,1024]{1,0:T(8,128)(2,1)} %param.8) | data formatting | bytes 4194304 | tf_op args[0]
  17.3 34.8 %while.12 = (s32[]{:T(128)}, f32[8,1024,128]{1,2,0:T(8,128)}, bf16[8,1024,128]{1,2,0:T(8,128)(2,1)S(1)}, bf16[8,1024,128]{1,2,0:T(8,128)(2,1)}, f32[8,1024,16]{1...) while((s32[]{:T(128)}, f32[8,1024,128]{1,2,0:T(8,128)}, ...), condition=%wide.region_1.2_spmd.clone.clone, body=%wide.region_0.1_spmd.clone.clone.sunk | while | flops 606076928 | bytes 1579089 | solution.py:68
  18.0 3.7 %fusion.97 = f32[8,1024,128]{1,2,0:T(8,128)} fusion(f32[8,1024,128]{1,2,0:T(8,128)} %get-tuple-element.235, s32[]{:T(128)} %get-tuple-element.234, f32[1024]{0:T(1024)S(1)} %bitcast.151, f32[1024]{0:T(1024)S(1)} %bitcast.152, f32[1024]{0:T(1024)S(1)} %bitcast.153, f32[1024]{0:T(1024)} %bitcast.154, f32[1024]{0:T(1024)} %bitcast.155, ...), kind=kOutput, calls=%fused_computation.18.clone.1 | convolution fusion | flops 606076928 | bytes 1357824 | tf_op jit(solution)/shard_map/while/body/eval_jaxpr/dot_general | solution.py:32
  22.3 3.7 %fusion.97 = f32[8,1024,128]{1,2,0:T(8,128)} fusion(f32[8,1024,128]{1,2,0:T(8,128)} %get-tuple-element.235, s32[]{:T(128)} %get-tuple-element.234, f32[1024]{0:T(1024)S(1)} %bitcast.151, f32[1024]{0:T(1024)S(1)} %bitcast.152, f32[1024]{0:T(1024)S(1)} %bitcast.153, f32[1024]{0:T(1024)} %bitcast.154, f32[1024]{0:T(1024)} %bitcast.155, ...), kind=kOutput, calls=%fused_computation.18.clone.1 | convolution fusion | flops 606076928 | bytes 1357824 | tf_op jit(solution)/shard_map/while/body/eval_jaxpr/dot_general | solution.py:32
  26.7 3.8 %fusion.97 = f32[8,1024,128]{1,2,0:T(8,128)} fusion(f32[8,1024,128]{1,2,0:T(8,128)} %get-tuple-element.235, s32[]{:T(128)} %get-tuple-element.234, f32[1024]{0:T(1024)S(1)} %bitcast.151, f32[1024]{0:T(1024)S(1)} %bitcast.152, f32[1024]{0:T(1024)S(1)} %bitcast.153, f32[1024]{0:T(1024)} %bitcast.154, f32[1024]{0:T(1024)} %bitcast.155, ...), kind=kOutput, calls=%fused_computation.18.clone.1 | convolution fusion | flops 606076928 | bytes 1357824 | tf_op jit(solution)/shard_map/while/body/eval_jaxpr/dot_general | solution.py:32
  31.1 3.7 %fusion.97 = f32[8,1024,128]{1,2,0:T(8,128)} fusion(f32[8,1024,128]{1,2,0:T(8,128)} %get-tuple-element.235, s32[]{:T(128)} %get-tuple-element.234, f32[1024]{0:T(1024)S(1)} %bitcast.151, f32[1024]{0:T(1024)S(1)} %bitcast.152, f32[1024]{0:T(1024)S(1)} %bitcast.153, f32[1024]{0:T(1024)} %bitcast.154, f32[1024]{0:T(1024)} %bitcast.155, ...), kind=kOutput, calls=%fused_computation.18.clone.1 | convolution fusion | flops 606076928 | bytes 1357824 | tf_op jit(solution)/shard_map/while/body/eval_jaxpr/dot_general | solution.py:32
  35.4 3.7 %fusion.97 = f32[8,1024,128]{1,2,0:T(8,128)} fusion(f32[8,1024,128]{1,2,0:T(8,128)} %get-tuple-element.235, s32[]{:T(128)} %get-tuple-element.234, f32[1024]{0:T(1024)S(1)} %bitcast.151, f32[1024]{0:T(1024)S(1)} %bitcast.152, f32[1024]{0:T(1024)S(1)} %bitcast.153, f32[1024]{0:T(1024)} %bitcast.154, f32[1024]{0:T(1024)} %bitcast.155, ...), kind=kOutput, calls=%fused_computation.18.clone.1 | convolution fusion | flops 606076928 | bytes 1357824 | tf_op jit(solution)/shard_map/while/body/eval_jaxpr/dot_general | solution.py:32
  39.8 3.7 %fusion.97 = f32[8,1024,128]{1,2,0:T(8,128)} fusion(f32[8,1024,128]{1,2,0:T(8,128)} %get-tuple-element.235, s32[]{:T(128)} %get-tuple-element.234, f32[1024]{0:T(1024)S(1)} %bitcast.151, f32[1024]{0:T(1024)S(1)} %bitcast.152, f32[1024]{0:T(1024)S(1)} %bitcast.153, f32[1024]{0:T(1024)} %bitcast.154, f32[1024]{0:T(1024)} %bitcast.155, ...), kind=kOutput, calls=%fused_computation.18.clone.1 | convolution fusion | flops 606076928 | bytes 1357824 | tf_op jit(solution)/shard_map/while/body/eval_jaxpr/dot_general | solution.py:32
  44.1 3.7 %fusion.97 = f32[8,1024,128]{1,2,0:T(8,128)} fusion(f32[8,1024,128]{1,2,0:T(8,128)} %get-tuple-element.235, s32[]{:T(128)} %get-tuple-element.234, f32[1024]{0:T(1024)S(1)} %bitcast.151, f32[1024]{0:T(1024)S(1)} %bitcast.152, f32[1024]{0:T(1024)S(1)} %bitcast.153, f32[1024]{0:T(1024)} %bitcast.154, f32[1024]{0:T(1024)} %bitcast.155, ...), kind=kOutput, calls=%fused_computation.18.clone.1 | convolution fusion | flops 606076928 | bytes 1357824 | tf_op jit(solution)/shard_map/while/body/eval_jaxpr/dot_general | solution.py:32
  48.5 3.7 %fusion.97 = f32[8,1024,128]{1,2,0:T(8,128)} fusion(f32[8,1024,128]{1,2,0:T(8,128)} %get-tuple-element.235, s32[]{:T(128)} %get-tuple-element.234, f32[1024]{0:T(1024)S(1)} %bitcast.151, f32[1024]{0:T(1024)S(1)} %bitcast.152, f32[1024]{0:T(1024)S(1)} %bitcast.153, f32[1024]{0:T(1024)} %bitcast.154, f32[1024]{0:T(1024)} %bitcast.155, ...), kind=kOutput, calls=%fused_computation.18.clone.1 | convolution fusion | flops 606076928 | bytes 1357824 | tf_op jit(solution)/shard_map/while/body/eval_jaxpr/dot_general | solution.py:32
  53.1 2.5 %collective-permute-start.1 = (bf16[8,128,128]{2,1,0:T(8,128)(2,1)S(1)}, bf16[8,128,128]{2,1,0:T(8,128)(2,1)S(1)}, u32[]{:S(2)}, u32[]{:S(2)}) collective-permute-start(bf16[8,128,128]{2,1,0:T(8,128)(2,1)S(1)} %fusion.62), channel_id=1, source_target_pairs={{0,16},{8,24},{16,0},{24,8},{32,48},{40,56},{48,32},{56,40},{64,80... | collective-permute-start | bytes 786440 | tf_op jit(solution)/shard_map/ppermute | solution.py:11
  56.4 5.0 %collective-permute-done.1 = bf16[8,128,128]{2,1,0:T(8,128)(2,1)S(1)} collective-permute-done((bf16[8,128,128]{2,1,0:T(8,128)(2,1)S(1)}, bf16[8,128,128]{2,1,0:T(8,128)(2,1)S(1)}, u32[]{:S(2)}, u32[]{:S(2)}) %collective-permute-start.1) | collective-permute-done | bytes 262176 | tf_op jit(solution)/shard_map/ppermute | solution.py:11
  64.1 4.0 %collective-permute-done.2 = bf16[8,128,128]{2,1,0:T(8,128)(2,1)S(1)} collective-permute-done((bf16[8,128,128]{2,1,0:T(8,128)(2,1)S(1)}, bf16[8,128,128]{2,1,0:T(8,128)(2,1)S(1)}, u32[]{:S(2)}, u32[]{:S(2)}) %collective-permute-start.2) | collective-permute-done | bytes 262176 | tf_op jit(solution)/shard_map/ppermute | solution.py:11
  68.3 3.1 %collective-permute-start.3 = (bf16[8,128,128]{2,1,0:T(8,128)(2,1)S(1)}, bf16[8,128,128]{2,1,0:T(8,128)(2,1)S(1)}, u32[]{:S(2)}, u32[]{:S(2)}) collective-permute-start(bf16[8,128,128]{2,1,0:T(8,128)(2,1)S(1)} %fusion.63), channel_id=1, source_target_pairs={{0,64},{8,72},{16,80},{24,88},{32,96},{40,104},{48,112},{56,120},{... | collective-permute-start | bytes 786440 | tf_op jit(solution)/shard_map/ppermute | solution.py:11
  72.1 10.6 %collective-permute-done.3 = bf16[8,128,128]{2,1,0:T(8,128)(2,1)S(1)} collective-permute-done((bf16[8,128,128]{2,1,0:T(8,128)(2,1)S(1)}, bf16[8,128,128]{2,1,0:T(8,128)(2,1)S(1)}, u32[]{:S(2)}, u32[]{:S(2)}) %collective-permute-start.3) | collective-permute-done | bytes 262176 | tf_op jit(solution)/shard_map/ppermute | solution.py:11
  82.9 6.5 %collective-permute-start.4 = (bf16[8,128,128]{2,1,0:T(8,128)(2,1)S(1)}, bf16[8,128,128]{2,1,0:T(8,128)(2,1)S(1)}, u32[]{:S(2)}, u32[]{:S(2)}) collective-permute-start(bf16[8,128,128]{2,1,0:T(8,128)(2,1)S(1)} %fusion.61), channel_id=1, source_target_pairs={{0,128},{8,136},{16,144},{24,152},{32,160},{40,168},{48,176},{56,1... | collective-permute-start | bytes 786440 | tf_op jit(solution)/shard_map/ppermute | solution.py:11
  90.2 7.9 %collective-permute-done.4 = bf16[8,128,128]{2,1,0:T(8,128)(2,1)S(1)} collective-permute-done((bf16[8,128,128]{2,1,0:T(8,128)(2,1)S(1)}, bf16[8,128,128]{2,1,0:T(8,128)(2,1)S(1)}, u32[]{:S(2)}, u32[]{:S(2)}) %collective-permute-start.4) | collective-permute-done | bytes 262176 | tf_op jit(solution)/shard_map/ppermute | solution.py:11
  98.1 4.1 %fusion.52 = bf16[1024,8,128]{0,2,1:T(8,128)(2,1)S(1)} fusion(f32[8,128,1024]{2,1,0:T(8,128)S(1)} %fusion.64, f32[8,128,1024]{2,1,0:T(8,128)S(1)} %fusion.66, f32[8,128,1024]{2,1,0:T(8,128)S(1)} %fusion.68, f32[8,128,1024]{2,1,0:T(8,128)S(1)} %fusion.70, f32[8,1024,128]{1,2,0:T(8,128)} %get-tuple-element.77, bf16[1024,8,128]{0,2,1:T(8,128)(2,1)S(1)} %bitcast.139, ...), kind=kOutput, calls=%fused_computation.53 | convolution fusion | flops 280363008 | bytes 25591812 | tf_op jit(solution)/shard_map/che,hef->chf/dot_general | solution.py:57
  103.2 34.8 %all_to_all.10 = bf16[8,128,1024]{1,2,0:T(8,128)(2,1)S(1)} all-to-all(bf16[8,128,1024]{1,2,0:T(8,128)(2,1)S(1)} %copy.55), channel_id=1, replica_groups=mesh['seq'=32,'head'=8] {'head'}, dimensions={0} | all-to-all | bytes 4194304 | tf_op jit(solution)/shard_map/all_to_all | solution.py:79
  140.2 5.6 %copy.56 = f32[128,8192]{1,0:T(8,128)} copy(f32[128,8192]{0,1:T(8,128)} %bitcast.140) | data formatting | bytes 8388608 | tf_op jit(solution)/shard_map/convert_element_type | solution.py:79
  146.9 5.6 %fusion.56 = bf16[128,8192]{1,0:T(8,128)(2,1)} fusion(bf16[128,8192]{1,0:T(8,128)(2,1)} %param.12, f32[128,8192]{1,0:T(8,128)} %copy.56, f32[8192]{0:T(1024)S(1)} %copy-done.1, f32[128]{0:T(128)S(1)} %add_rsqrt_fusion), kind=kLoop, calls=%fused_computation.62 | loop fusion | flops 9437184 | bytes 8421888 | tf_op jit(solution)/shard_map/convert_element_type | solution.py:84
  (42 shorter events, 19.5 us)
Async XLA Ops:
  2.9 7.6 %copy-start = (bf16[1024,1024]{0,1:T(8,128)(2,1)}, bf16[1024,1024]{0,1:T(8,128)(2,1)S(1)}, u32[]{:S(2)}) copy-start(bf16[1024,1024]{0,1:T(8,128)(2,1)S(1)} %copy.37) | copy-start | bytes 6291460
  10.5 42.5 %collective-permute-start = (bf16[8,128,128]{2,1,0:T(8,128)(2,1)}, bf16[8,128,128]{2,1,0:T(8,128)(2,1)S(1)}, u32[]{:S(2)}, u32[]{:S(2)}) collective-permute-start(bf16[8,128,128]{2,1,0:T(8,128)(2,1)} %get-tuple-element.162), channel_id=1, source_target_pairs={{0,8},{8,0},{16,24},{24,16},{32,40},{40,32},{48,56},{56,48},{64,72... | collective-permute-start | bytes 786440 | tf_op jit(solution)/shard_map/ppermute | solution.py:11
  53.1 8.3 %collective-permute-start.1 = (bf16[8,128,128]{2,1,0:T(8,128)(2,1)S(1)}, bf16[8,128,128]{2,1,0:T(8,128)(2,1)S(1)}, u32[]{:S(2)}, u32[]{:S(2)}) collective-permute-start(bf16[8,128,128]{2,1,0:T(8,128)(2,1)S(1)} %fusion.62), channel_id=1, source_target_pairs={{0,16},{8,24},{16,0},{24,8},{32,48},{40,56},{48,32},{56,40},{64,80... | collective-permute-start | bytes 786440 | tf_op jit(solution)/shard_map/ppermute | solution.py:11
  61.5 6.7 %collective-permute-start.2 = (bf16[8,128,128]{2,1,0:T(8,128)(2,1)S(1)}, bf16[8,128,128]{2,1,0:T(8,128)(2,1)S(1)}, u32[]{:S(2)}, u32[]{:S(2)}) collective-permute-start(bf16[8,128,128]{2,1,0:T(8,128)(2,1)S(1)} %fusion.77), channel_id=1, source_target_pairs={{0,32},{8,40},{16,48},{24,56},{32,0},{40,8},{48,16},{56,24},{64,96... | collective-permute-start | bytes 786440 | tf_op jit(solution)/shard_map/ppermute | solution.py:11
  68.3 14.5 %collective-permute-start.3 = (bf16[8,128,128]{2,1,0:T(8,128)(2,1)S(1)}, bf16[8,128,128]{2,1,0:T(8,128)(2,1)S(1)}, u32[]{:S(2)}, u32[]{:S(2)}) collective-permute-start(bf16[8,128,128]{2,1,0:T(8,128)(2,1)S(1)} %fusion.63), channel_id=1, source_target_pairs={{0,64},{8,72},{16,80},{24,88},{32,96},{40,104},{48,112},{56,120},{... | collective-permute-start | bytes 786440 | tf_op jit(solution)/shard_map/ppermute | solution.py:11
  82.9 15.2 %collective-permute-start.4 = (bf16[8,128,128]{2,1,0:T(8,128)(2,1)S(1)}, bf16[8,128,128]{2,1,0:T(8,128)(2,1)S(1)}, u32[]{:S(2)}, u32[]{:S(2)}) collective-permute-start(bf16[8,128,128]{2,1,0:T(8,128)(2,1)S(1)} %fusion.61), channel_id=1, source_target_pairs={{0,128},{8,136},{16,144},{24,152},{32,160},{40,168},{48,176},{56,1... | collective-permute-start | bytes 786440 | tf_op jit(solution)/shard_map/ppermute | solution.py:11
  140.2 6.7 %copy-start.1 = (f32[8192]{0:T(1024)S(1)}, f32[8192]{0:T(1024)}, u32[]{:S(2)}) copy-start(f32[8192]{0:T(1024)} %param.13) | copy-start | bytes 98308
where the time goes:
time: 153 us; the launch traced here: 152 us
  matrix products  39.9 us (26%)
  blocking collectives  34.8 us (23%)
  waiting for transfers between devices  27.5 us (18%)
  local copies, waits for them, and re-layouts  24.7 us (16%)
  starting transfers between devices  16.1 us (11%)
  other arithmetic  9.37 us (6%)
    all_to_all x1, blocking collectives, per_device(): lax.all_to_all(attended, 'head', split_axis=0, concat_axis=1, tiled=True)  34.8 us
    dot_general x8, matrix products, local_attention(): return jnp.dot(weighted, value_head, preferred_element_type=jnp.float32)  29.7 us
    ppermute x5, waiting for transfers between devices, swapped(): lax.ppermute(array, axis, [(i, i ^ 1 << bit) for i in range(lax.axis_size...  27.5 us
    ppermute x5, starting transfers between devices, swapped(): lax.ppermute(array, axis, [(i, i ^ 1 << bit) for i in range(lax.axis_size...  16.1 us
    unnamed x12, local copies, waits for them, and re-layouts  13 us
    dot_general x5, matrix products, per_device(): jnp.einsum('che,hef->chf', query_rows, rounded[height], preferred_element...  7.13 us
    convert_element_type x1, local copies, waits for them, and re-layouts, per_device(): lax.all_to_all(attended, 'head', split_axis=0, concat_axis=1, tiled=True)  5.62 us
    convert_element_type x1, other arithmetic, per_device(): (token_rows * lax.rsqrt(mean_square + 1e-06) * norm_gain[None, :] * gatin...  5.58 us
  transfers between devices with their start and end apart: 5, of which 4 were waited for; matrix products, arithmetic and copies ran while one was open for 28% of the time, Pallas kernels for 0%

commit v1 on v0

v1 whole, which is shorter than its diff:
```python
import functools
import jax
import jax.numpy as jnp
from jax import lax
from jax.experimental import pallas as pl
from jax.experimental.pallas import tpu as pltpu
from jax.sharding import PartitionSpec as P

HEAD_DIM = 128
LEVELS = 16
CHUNK = 128
MESH = pl.DeviceIdType.MESH
F32 = jnp.float32
BF16 = jnp.bfloat16


def partner_masks(n_seq):
    masks = {32: (1, 3, 4, 8, 28)}
    return masks.get(n_seq, tuple(1 << b for b in range(n_seq.bit_length() - 1)))


def kernel(
    n_seq, n_head, q_hbm, k_hbm, v_hbm, w_hbm, gate_hbm, gain_hbm, out_hbm,
    qb, kb, vb, wb, gateb, gainb, gsb, levb, inner, wq, tiers, run, sbuf, loc, att, rows, outb, sumsq,
    q_sem, k_sem, v_sem, w_sem, gate_sem, gain_sem, out_sem,
    xs_sem, xr_sem, as_sem, ar_sem,
):
    masks = partner_masks(n_seq)
    steps = len(masks)
    heads = qb.shape[0]
    count = qb.shape[1]
    chunks = count // CHUNK
    chunk_bits = CHUNK.bit_length() - 1
    local_bits = count.bit_length() - 1
    tokens_out = rows.shape[1]
    me_seq = lax.axis_index("seq")
    me_head = lax.axis_index("head")

    def columns(h):
        return pl.ds(pl.multiple_of(h * HEAD_DIM, HEAD_DIM), HEAD_DIM)

    def load_k(h):
        return pltpu.make_async_copy(k_hbm.at[:, columns(h)], kb.at[h], k_sem.at[h])

    def load_v(h):
        return pltpu.make_async_copy(v_hbm.at[:, columns(h)], vb.at[h], v_sem.at[h])

    def load_q(h):
        return pltpu.make_async_copy(q_hbm.at[:, columns(h)], qb.at[h], q_sem.at[h])

    load_w = pltpu.make_async_copy(w_hbm, wb, w_sem)
    load_gate = pltpu.make_async_copy(gate_hbm, gateb, gate_sem)
    load_gain = pltpu.make_async_copy(gain_hbm, gainb, gain_sem)

    def tier_of(s, h):
        return tiers.at[h, s * HEAD_DIM : (s + 1) * HEAD_DIM, :]

    def exchange(s, h):
        return pltpu.make_async_remote_copy(
            src_ref=sbuf.at[s, h],
            dst_ref=tier_of(s, h),
            send_sem=xs_sem.at[s, h],
            recv_sem=xr_sem.at[s, h],
            device_id={"seq": me_seq ^ masks[s]},
            device_id_type=MESH,
        )

    def tokens_of(j):
        return pl.ds(pl.multiple_of(j * tokens_out, tokens_out), tokens_out)

    def scatter(k, h):
        to = me_head ^ k
        return pltpu.make_async_remote_copy(
            src_ref=att.at[h, tokens_of(to), :],
            dst_ref=rows.at[me_head * heads + h],
            send_sem=as_sem.at[k, h],
            recv_sem=ar_sem.at[k, h],
            device_id={"head": to},
            device_id_type=MESH,
        )

    def keep(h):
        return pltpu.make_async_copy(
            att.at[h, tokens_of(me_head), :], rows.at[me_head * heads + h], as_sem.at[0, h]
        )

    barrier = pltpu.get_barrier_semaphore()
    for mask in masks:
        pl.semaphore_signal(barrier, inc=1, device_id={"seq": me_seq ^ mask}, device_id_type=MESH)
    for k in range(1, n_head):
        pl.semaphore_signal(barrier, inc=1, device_id={"head": me_head ^ k}, device_id_type=MESH)

    @pl.loop(0, heads)
    def _(h):
        load_k(h).start()
        load_v(h).start()

    load_w.start()

    @pl.loop(0, heads)
    def _(h):
        load_q(h).start()

    load_gate.start()
    load_gain.start()

    t_id = lax.broadcasted_iota(jnp.int32, (CHUNK, CHUNK), 0)
    s_id = lax.broadcasted_iota(jnp.int32, (CHUNK, CHUNK), 1)
    mixed = t_id ^ s_id
    level = jnp.zeros((CHUNK, CHUNK), jnp.int32)
    for height in range(chunk_bits):
        level = level + (mixed >= 1 << height).astype(jnp.int32)
    levb[...] = level
    sumsq[...] = jnp.zeros_like(sumsq)

    def part(h, c):
        at = slice(c * CHUNK, (c + 1) * CHUNK)
        return lax.dot_general(
            kb[h, at, :], vb[h, at, :], (((0,), (0,)), ((), ())), preferred_element_type=F32
        )

    def span_sum(h, first, size):
        if size == 1:
            return part(h, first)
        half = size // 2
        left = span_sum(h, first, half)
        loc[h, loc_slot(first, half)] = left.astype(BF16)
        return left + span_sum(h, first + half, half)

    def loc_slot(first, half):
        base, size = 0, 1
        while size < half:
            base += chunks // (2 * size)
            size *= 2
        return base + first // (2 * half)

    @pl.loop(0, heads)
    def _(h):
        load_k(h).wait()
        load_v(h).wait()
        total = span_sum(h, 0, chunks)
        run[h] = total
        sbuf[0, h] = total.astype(BF16)

        @pl.when(h == 0)
        def _():
            pl.semaphore_wait(barrier, steps + n_head - 1)

        exchange(0, h).start()

    load_w.wait()
    slot = lax.broadcasted_iota(jnp.int32, (1, wb.shape[1]), 1) & (LEVELS - 1)
    taken = jnp.ones((1, wb.shape[1]), F32)
    for s in range(steps):
        bit = (lax.shift_right_logical(me_seq, s) & 1).astype(F32)
        taken = jnp.where(slot == local_bits + 1 + s, bit, taken)
    wb[...] = wb[...] * taken

    def inside(h):
        load_q(h).wait()
        pick = levb[...] + h * LEVELS
        causal = lax.broadcasted_iota(jnp.int32, (CHUNK, CHUNK), 1) <= lax.broadcasted_iota(
            jnp.int32, (CHUNK, CHUNK), 0
        )
        for c in range(chunks):
            at = slice(c * CHUNK, (c + 1) * CHUNK)
            q_c = qb[h, at, :]
            w_c = wb[at, :]
            q_f = q_c.astype(F32)

            def weighted_q(lev):
                w_l = jnp.take_along_axis(
                    w_c, jnp.full((CHUNK, CHUNK), h * LEVELS + lev, jnp.int32), axis=1
                )
                return (q_f * w_l).astype(BF16)

            scores = lax.dot_general(
                q_c, kb[h, at, :], (((1,), (1,)), ((), ())), preferred_element_type=F32
            )
            factor = jnp.take_along_axis(w_c, pick, axis=1)
            left = [jnp.where(causal, scores * factor, F32(0.0)).astype(BF16)]
            right = [vb[h, at, :]]
            for b in range(chunks.bit_length() - 1):
                if c >> b & 1:
                    left.append(weighted_q(chunk_bits + 1 + b))
                    right.append(loc[h, loc_slot((c >> b << b) - (1 << b), 1 << b)])
            inner[h, at, :] = jnp.dot(
                jnp.concatenate(left, axis=1),
                jnp.concatenate(right, axis=0),
                preferred_element_type=F32,
            )
            for s in range(steps):
                wq[h, at, s * HEAD_DIM : (s + 1) * HEAD_DIM] = weighted_q(local_bits + 1 + s)

    def service(s, h):
        exchange(s, h).wait_recv()
        if s < steps - 1:
            total = run[h] + tier_of(s, h)[...].astype(F32)
            run[h] = total
            sbuf[s + 1, h] = total.astype(BF16)
            exchange(s + 1, h).start()
            return
        cross = jnp.dot(wq[h], tiers[h], preferred_element_type=F32)
        att[h] = (inner[h] + cross).astype(BF16)
        for k in range(1, n_head):
            scatter(k, h).start()
        keep(h).start()

    lag = 2

    @pl.loop(0, heads + lag * (steps - 1) + 1)
    def _(i):
        @pl.when(i < heads)
        def _():
            inside(jnp.minimum(i, heads - 1))

        for s in range(steps):
            h = i - 1 - lag * s if s < steps - 1 else i - lag * s - 1

            @pl.when((h >= 0) & (h < heads))
            def _(s=s, h=h):
                service(s, h)

    load_gate.wait()
    load_gain.wait()

    wide = n_head * HEAD_DIM

    @pl.loop(0, heads)
    def _(h):
        at = pl.ds(pl.multiple_of(h * wide, wide), wide)
        gate = gateb[:, at].astype(F32)
        gsb[:, at] = gainb[:, at] * (gate / (1.0 + jnp.exp(-gate)))
        keep(h).wait()
        for k in range(1, n_head):
            scatter(k, h).wait_recv()
        total = sumsq[...]
        for j in range(n_head):
            x = rows[j * heads + h].astype(F32)
            total = total + x * x
        sumsq[...] = total

    mean_square = jnp.sum(sumsq[...], axis=1, keepdims=True) * (1.0 / (heads * n_head * HEAD_DIM))
    scale = jnp.broadcast_to(lax.rsqrt(mean_square + 1e-06), (tokens_out, HEAD_DIM))
    sumsq[...] = scale

    def store(j):
        span = heads * HEAD_DIM
        return pltpu.make_async_copy(
            outb.at[j], out_hbm.at[:, pl.ds(pl.multiple_of(j * span, span), span)], out_sem.at[j]
        )

    @pl.loop(0, n_head)
    def _(j):
        for u in range(heads):
            at = pl.ds(pl.multiple_of((j * heads + u) * HEAD_DIM, HEAD_DIM), HEAD_DIM)
            x = rows[j * heads + u].astype(F32)
            outb[j, :, u * HEAD_DIM : (u + 1) * HEAD_DIM] = (x * sumsq[...] * gsb[:, at]).astype(BF16)
        store(j).start()

    @pl.loop(0, n_head)
    def _(j):
        store(j).wait()

    @pl.loop(0, heads)
    def _(h):
        for s in range(steps):
            exchange(s, h).wait_send()
        for k in range(1, n_head):
            scatter(k, h).wait_send()


def per_device(queries, key_vectors, value_vectors, level_weight, gate_values, norm_gain):
    count, features = queries.shape
    heads = features // HEAD_DIM
    n_seq, n_head = lax.axis_size("seq"), lax.axis_size("head")
    steps = n_seq.bit_length() - 1
    tokens_out, width = gate_values.shape
    chunks = count // CHUNK
    vmem, dma = pltpu.VMEM, pltpu.SemaphoreType.DMA
    return pl.pallas_call(
        functools.partial(kernel, n_seq, n_head),
        out_shape=jax.ShapeDtypeStruct((tokens_out, width), BF16),
        in_specs=[pl.BlockSpec(memory_space=pl.ANY)] * 6,
        out_specs=pl.BlockSpec(memory_space=pl.ANY),
        scratch_shapes=[
            vmem((heads, count, HEAD_DIM), BF16),
            vmem((heads, count, HEAD_DIM), BF16),
            vmem((heads, count, HEAD_DIM), BF16),
            vmem((count, heads * LEVELS), F32),
            vmem((tokens_out, width), BF16),
            vmem((1, width), F32),
            vmem((tokens_out, width), F32),
            vmem((CHUNK, CHUNK), jnp.int32),
            vmem((heads, count, HEAD_DIM), F32),
            vmem((heads, count, steps * HEAD_DIM), BF16),
            vmem((heads, steps * HEAD_DIM, HEAD_DIM), BF16),
            vmem((heads, HEAD_DIM, HEAD_DIM), F32),
            vmem((steps, heads, HEAD_DIM, HEAD_DIM), BF16),
            vmem((heads, chunks - 1, HEAD_DIM, HEAD_DIM), BF16),
            vmem((heads, count, HEAD_DIM), BF16),
            vmem((n_head * heads, tokens_out, HEAD_DIM), BF16),
            vmem((n_head, tokens_out, heads * HEAD_DIM), BF16),
            vmem((tokens_out, HEAD_DIM), F32),
            dma((heads,)),
            dma((heads,)),
            dma((heads,)),
            dma,
            dma,
            dma,
            dma((n_head,)),
            dma((steps, heads)),
            dma((steps, heads)),
            dma((n_head, heads)),
            dma((n_head, heads)),
        ],
        compiler_params=pltpu.CompilerParams(
            collective_id=0, has_side_effects=True, vmem_limit_bytes=60 << 20
        ),
    )(queries, key_vectors, value_vectors, level_weight, gate_values, norm_gain[None, :])


def solution(mesh):
    placed = (
        P("seq", "head"),
        P("seq", "head"),
        P("seq", "head"),
        P("seq", "head"),
        P(("seq", "head"), None),
        P(),
    )
    return jax.shard_map(
        per_device, mesh=mesh, in_specs=placed, out_specs=P(("seq", "head"), None), check_vma=False
    )
```

time: 153 us -> 61.2 us (0.40)
  the two profiles are of different devices: /device:TPU:1 before, /device:TPU:33 now
where the time goes in v1:
time: 61.2 us; the launch traced here: 61.1 us
  Pallas kernels  58 us (95%)
  local copies, waits for them, and re-layouts  3.1 us (5%)
    pallas_call x1, Pallas kernels, per_device(): pl.pallas_call(functools.partial(kernel, n_seq, n_head), out_shape=jax.Sh...  58 us
    unnamed x1, local copies, waits for them, and re-layouts  3.1 us

profile of v1, /device:TPU:33, one launch (start us, length us, event | category | flops | bytes accessed | tf_op | source)
XLA Modules:
  0.0 61.1 jit_solution(18044353848301324933)
XLA Ops:
  0.0 58.0 %shard_map.64 = bf16[128,8192]{1,0:T(8,128)(2,1)} custom-call(bf16[1024,1024]{1,0:T(8,128)(2,1)} %q_hbm.1, bf16[1024,1024]{1,0:T(8,128)(2,1)} %k_hbm.1, bf16[1024,1024]{1,0:T(8,128)(2,1)} %v_hbm.1, f32[1024,128]{1,0:T(8,128)} %w_hbm.1, bf16[128,8192]{1,0:T(8,128)(2,1)} %gate_hbm.1, f32[1,8192]{1,0:T(1,128)} %bitcast.1), custom_call_target="tpu_custom_call" | custom-call | tf_op jit(solution)/shard_map/pallas_call | solution.py:281
  58.0 3.1 %copy.8 = bf16[128,8192]{1,0:T(8,128)(2,1)} copy(bf16[128,8192]{1,0:T(8,128)(2,1)} %shard_map.64) | data formatting | bytes 4194304

commit v2 on v1

v2 whole, which is shorter than its diff:
```python
import functools
import jax
import jax.numpy as jnp
from jax import lax
from jax.experimental import pallas as pl
from jax.experimental.pallas import tpu as pltpu
from jax.sharding import PartitionSpec as P

HEAD_DIM = 128
LEVELS = 16
CHUNK = 128
MESH = pl.DeviceIdType.MESH
F32 = jnp.float32
BF16 = jnp.bfloat16


PLAN = ((1, 2, 3), (4, 8, 12), (28, 24))
PARTS = 2
DUE = ((1, 2), (6, 3), (11, 4))
FAR_FIRST = (4, 5, 2, 3, 6, 7, 1)


def kernel(
    n_seq, n_head, q_hbm, k_hbm, v_hbm, w_hbm, gate_hbm, gain_hbm, out_ref,
    qb, kb, vb, wb, wlow, spread, gateb, gainb, gsb, levb, inner, wq, tiers, xbuf, run, sbuf, loc, att, rows, sumsq,
    q_sem, k_sem, v_sem, w_sem, gate_sem, gain_sem,
    xs_sem, xr_sem, ready, ys_sem, yr_sem, keep_sem,
):
    plan = PLAN
    steps = len(plan)
    levels_out = n_seq.bit_length() - 1
    heads = qb.shape[0]
    count = qb.shape[1]
    chunks = count // CHUNK
    chunk_bits = CHUNK.bit_length() - 1
    local_bits = count.bit_length() - 1
    tokens_out = sumsq.shape[0]
    me_seq = lax.axis_index("seq")
    me_head = lax.axis_index("head")

    def columns(h):
        return pl.ds(pl.multiple_of(h * HEAD_DIM, HEAD_DIM), HEAD_DIM)

    def load_k(h):
        return pltpu.make_async_copy(k_hbm.at[:, columns(h)], kb.at[h], k_sem.at[h])

    def load_v(h):
        return pltpu.make_async_copy(v_hbm.at[:, columns(h)], vb.at[h], v_sem.at[h])

    def load_q(h):
        return pltpu.make_async_copy(q_hbm.at[:, columns(h)], qb.at[h], q_sem.at[h])

    load_w = pltpu.make_async_copy(w_hbm, wb, w_sem)
    load_gate = pltpu.make_async_copy(gate_hbm, gateb, gate_sem)
    load_gain = pltpu.make_async_copy(gain_hbm, gainb, gain_sem)

    def tier_of(m, h):
        return tiers.at[h, m * HEAD_DIM : (m + 1) * HEAD_DIM, :]

    def landing(s, j, h):
        return tier_of(2 * s, h) if j == 0 or s == 2 else xbuf.at[2 * s + j - 1, h]

    me_z = lax.shift_right_logical(me_seq, 2)
    in_four = me_z & 3
    upper = me_z >= 4

    def upward(j):
        return (in_four ^ (j + 1)) > in_four

    def downward(j):
        return (me_z ^ (j + 1)) == 0

    def sends(s, j):
        if s == 1:
            return upward(j) | downward(j)
        return (me_z == 0) | (me_z == 3)

    def receives(s, j):
        if s == 1:
            return ((in_four ^ (j + 1)) < in_four) | (me_z == 0)
        near = (me_z == 4) | (me_z == 7) if j == 0 else (me_z == 5) | (me_z == 6)
        return near

    def start_exchange(s, j, h):
        if s == 0:
            exchange(s, j, h).start()
            return

        @pl.when(sends(s, j))
        def _():
            if s == 1:
                @pl.when((h == 0) & upward(j))
                def _():
                    pl.semaphore_wait(ready.at[j], 1)
            else:
                @pl.when(h == 0)
                def _():
                    pl.semaphore_wait(ready.at[3 + j], 1)
            exchange(s, j, h).start()

    def wait_exchange(s, j, h):
        if s == 0:
            exchange(s, j, h).wait_recv()
            return

        @pl.when(receives(s, j))
        def _():
            exchange(s, j, h).wait_recv()

    def row_partner(mask):
        return {"seq": me_seq ^ mask}

    def exchange(s, j, h):
        n = sum(len(p) for p in plan[:s]) + j
        return pltpu.make_async_remote_copy(
            src_ref=sbuf.at[s, h],
            dst_ref=landing(s, j, h),
            send_sem=xs_sem.at[n, h],
            recv_sem=xr_sem.at[n, h],
            device_id={"seq": me_seq ^ plan[s][j]},
            device_id_type=MESH,
        )

    def tokens_of(j):
        return pl.ds(pl.multiple_of(j * tokens_out, tokens_out), tokens_out)

    def scatter(k, h):
        return pltpu.make_async_remote_copy(
            src_ref=att.at[h, tokens_of(me_head ^ k), :],
            dst_ref=rows.at[me_head, h],
            send_sem=ys_sem.at[k, h],
            recv_sem=yr_sem.at[k, h],
            device_id={"head": me_head ^ k},
            device_id_type=MESH,
        )

    def keep(h):
        return pltpu.make_async_copy(att.at[h, tokens_of(me_head), :], rows.at[me_head, h], keep_sem.at[h])

    load_k(0).start()
    load_v(0).start()
    barrier = pltpu.get_barrier_semaphore()
    for mask in plan[0]:
        pl.semaphore_signal(barrier, inc=1, device_id=row_partner(mask), device_id_type=MESH)
    for k in range(1, n_head):
        pl.semaphore_signal(barrier, inc=1, device_id={"head": me_head ^ k}, device_id_type=MESH)

    for j, mask in enumerate(plan[1]):
        @pl.when(upward(j))
        def _(mask=mask):
            pl.semaphore_signal(barrier, inc=1, device_id=row_partner(mask), device_id_type=MESH)

    for j, mask in enumerate(plan[2]):
        @pl.when(sends(2, j))
        def _(mask=mask):
            pl.semaphore_signal(barrier, inc=1, device_id=row_partner(mask), device_id_type=MESH)

    @pl.loop(1, heads)
    def _(h):
        load_k(h).start()
        load_v(h).start()

    load_w.start()

    @pl.loop(0, heads)
    def _(h):
        load_q(h).start()

    load_gate.start()
    load_gain.start()

    t_id = lax.broadcasted_iota(jnp.int32, (CHUNK, CHUNK), 0)
    s_id = lax.broadcasted_iota(jnp.int32, (CHUNK, CHUNK), 1)
    mixed = t_id ^ s_id
    level = jnp.zeros((CHUNK, CHUNK), jnp.int32)
    for height in range(chunk_bits):
        level = level + (mixed >= 1 << height).astype(jnp.int32)
    levb[...] = level
    sumsq[...] = jnp.zeros_like(sumsq)

    @pl.loop(0, heads)
    def _(h):
        for s in (1, 2):
            for j in range(len(plan[s])):
                if s == 2 and j == 1:
                    continue
                empty = jnp.logical_not(receives(s, j)) if s == 1 else jnp.logical_not(upper)

                @pl.when(empty)
                def _(s=s, j=j):
                    landing(s, j, h)[...] = jnp.zeros((HEAD_DIM, HEAD_DIM), BF16)

    @pl.loop(0, heads)
    def _(h):
        row = lax.broadcasted_iota(jnp.int32, (spread.shape[1], HEAD_DIM), 0)
        for n in range(spread.shape[2] // HEAD_DIM):
            here = row == h * LEVELS + chunk_bits + 1 + n
            spread[h, :, n * HEAD_DIM : (n + 1) * HEAD_DIM] = jnp.where(here, F32(1.0), F32(0.0)).astype(BF16)

    def part(h, c):
        at = slice(c * CHUNK, (c + 1) * CHUNK)
        return lax.dot_general(
            kb[h, at, :], vb[h, at, :], (((0,), (0,)), ((), ())), preferred_element_type=F32
        )

    def loc_slot(first, half):
        base, size = 0, 1
        while size < half:
            base += chunks // (2 * size)
            size *= 2
        return base + first // (2 * half)

    def span_sum(h, first, size):
        if size == 1:
            return part(h, first)
        half = size // 2
        left = span_sum(h, first, half)
        loc[h, loc_slot(first, half)] = left.astype(BF16)
        return left + span_sum(h, first + half, half)

    @pl.loop(0, heads)
    def _(h):
        load_k(h).wait()
        load_v(h).wait()
        total = span_sum(h, 0, chunks)
        run[h] = total
        sbuf[0, h] = total.astype(BF16)

        @pl.when(h == 0)
        def _():
            pl.semaphore_wait(
                barrier, len(plan[0]) + n_head - 1 + in_four + jnp.where(upper, 1, 0)
            )
            for j, mask in enumerate(plan[1]):
                @pl.when((in_four ^ (j + 1)) < in_four)
                def _(j=j, mask=mask):
                    pl.semaphore_signal(
                        ready.at[j], inc=1, device_id=row_partner(mask), device_id_type=MESH
                    )

            for j, mask in enumerate(plan[2]):
                @pl.when(receives(2, j))
                def _(j=j, mask=mask):
                    pl.semaphore_signal(
                        ready.at[3 + j], inc=1, device_id=row_partner(mask), device_id_type=MESH
                    )

        for j in range(len(plan[0])):
            start_exchange(0, j, h)

    load_w.wait()
    slot = lax.broadcasted_iota(jnp.int32, (1, wb.shape[1]), 1) & (LEVELS - 1)
    taken = jnp.ones((1, wb.shape[1]), F32)
    for m in range(levels_out):
        bit = (lax.shift_right_logical(me_seq, m) & 1).astype(F32)
        taken = jnp.where(slot == local_bits + 1 + m, bit, taken)
    wlow[...] = (wb[...] * taken).astype(BF16)

    def inside(h, which):
        pick = levb[...] + h * LEVELS
        causal = lax.broadcasted_iota(jnp.int32, (CHUNK, CHUNK), 1) <= lax.broadcasted_iota(
            jnp.int32, (CHUNK, CHUNK), 0
        )
        which = list(which)
        base = which[0] * CHUNK
        span = slice(base, base + len(which) * CHUNK)
        inner_bits = chunks.bit_length() - 1

        def weighted_q(n, size, rows_at):
            spread_w = jnp.dot(
                wlow[rows_at, :],
                spread[h, :, n * HEAD_DIM : (n + size) * HEAD_DIM],
                preferred_element_type=F32,
            ).astype(BF16)
            q_rows = qb[h, rows_at, :]
            return [q_rows * spread_w[:, m * HEAD_DIM : (m + 1) * HEAD_DIM] for m in range(size)]

        scores = []
        for c in which:
            at = slice(c * CHUNK, (c + 1) * CHUNK)
            scores.append(
                lax.dot_general(
                    qb[h, at, :], kb[h, at, :], (((1,), (1,)), ((), ())), preferred_element_type=F32
                )
            )
        for n in range(0, levels_out, 2):
            size = min(2, levels_out - n)
            for m, scaled in enumerate(weighted_q(inner_bits + n, size, span)):
                wq[h, span, (n + m) * HEAD_DIM : (n + m + 1) * HEAD_DIM] = scaled
        lefts = []
        for c, score in zip(which, scores):
            at = slice(c * CHUNK, (c + 1) * CHUNK)
            factor = jnp.take_along_axis(wb[at, :], pick, axis=1)
            left = [jnp.where(causal, score * factor, F32(0.0)).astype(BF16)]
            bits = [n for n in range(inner_bits) if c >> n & 1]
            if bits == [0, 1]:
                left += weighted_q(0, 2, at)
            else:
                for n in bits:
                    left += weighted_q(n, 1, at)
            lefts.append((c, bits, left))
        for c, bits, left in lefts:
            at = slice(c * CHUNK, (c + 1) * CHUNK)
            right = [vb[h, at, :]] + [
                loc[h, loc_slot((c >> n << n) - (1 << n), 1 << n)] for n in bits
            ]
            inner[h, at, :] = jnp.dot(
                jnp.concatenate(left, axis=1),
                jnp.concatenate(right, axis=0),
                preferred_element_type=F32,
            )

    def service(s, h):
        for j in range(len(plan[s])):
            wait_exchange(s, j, h)
        pair = None
        if len(plan[s]) == 3:
            pair = xbuf[2 * s, h].astype(F32) + xbuf[2 * s + 1, h].astype(F32)
            tier_of(2 * s + 1, h)[...] = pair.astype(BF16)
        if s < steps - 1:
            total = run[h] + tier_of(2 * s, h)[...].astype(F32)
            if pair is not None:
                total = total + pair
            run[h] = total
            sbuf[s + 1, h] = total.astype(BF16)
            for j in range(len(plan[s + 1])):
                start_exchange(s + 1, j, h)
            return
        cross = jnp.dot(wq[h], tiers[h], preferred_element_type=F32)
        att[h] = (inner[h] + cross).astype(BF16)
        for k in FAR_FIRST:
            scatter(k, h).start()
        keep(h).start()

    wide = n_head * HEAD_DIM

    def gating(j):
        at = pl.ds(pl.multiple_of(j * wide, wide), wide)
        gate = gateb[:, at].astype(F32)
        gsb[:, at] = gainb[:, at] * (gate / (1.0 + jnp.exp(-gate)))

    def collect(h):
        keep(h).wait()
        for k in range(1, n_head):
            scatter(k, h).wait_recv()
        total = sumsq[...]
        for j in range(n_head):
            x = rows[j, h].astype(F32)
            total = total + x * x
        sumsq[...] = total

    units = PARTS * heads
    each = chunks // PARTS

    @pl.loop(0, max(units + heads, DUE[-1][0] + DUE[-1][1] * (heads - 1) + 1))
    def _(i):
        for n, (first, rate) in enumerate(DUE):
            h = (i - first) // rate

            @pl.when((i >= first) & (h < heads) & (lax.rem(i - first, rate) == 0))
            def _(n=n, h=h):
                service(n, h)

        for p in range(PARTS):
            @pl.when((i < units) & (lax.rem(i, PARTS) == p))
            def _(p=p):
                h = i // PARTS
                if p == 0:
                    load_q(h).wait()
                inside(h, range(p * each, (p + 1) * each))

        @pl.when(i == units)
        def _():
            load_gate.wait()
            load_gain.wait()

        @pl.when((i >= units) & (i < units + heads))
        def _():
            gating(i - units)

    @pl.loop(0, heads)
    def _(h):
        collect(h)

    mean_square = jnp.sum(sumsq[...], axis=1, keepdims=True) * (1.0 / (heads * n_head * HEAD_DIM))
    scale = jnp.broadcast_to(lax.rsqrt(mean_square + 1e-06), (tokens_out, HEAD_DIM))
    sumsq[...] = scale

    @pl.loop(0, n_head)
    def _(j):
        for h in range(heads):
            at = columns(j * heads + h)
            x = rows[j, h].astype(F32)
            out_ref[:, at] = (x * sumsq[...] * gsb[:, at]).astype(BF16)

    @pl.loop(0, heads)
    def _(h):
        for s in range(steps):
            for j in range(len(plan[s])):
                if s == 0:
                    exchange(s, j, h).wait_send()
                else:
                    @pl.when(sends(s, j))
                    def _(s=s, j=j):
                        exchange(s, j, h).wait_send()

        for k in range(1, n_head):
            scatter(k, h).wait_send()


def per_device(queries, key_vectors, value_vectors, level_weight, gate_values, norm_gain):
    count, features = queries.shape
    heads = features // HEAD_DIM
    n_seq, n_head = lax.axis_size("seq"), lax.axis_size("head")
    levels_out = n_seq.bit_length() - 1
    sends = sum(len(part) for part in PLAN)
    tokens_out, width = gate_values.shape
    chunks = count // CHUNK
    vmem, dma = pltpu.VMEM, pltpu.SemaphoreType.DMA
    return pl.pallas_call(
        functools.partial(kernel, n_seq, n_head),
        out_shape=pltpu.VMEM((tokens_out, width), BF16),
        in_specs=[pl.BlockSpec(memory_space=pl.ANY)] * 6,
        out_specs=pl.BlockSpec(memory_space=pltpu.VMEM),
        scratch_shapes=[
            vmem((heads, count, HEAD_DIM), BF16),
            vmem((heads, count, HEAD_DIM), BF16),
            vmem((heads, count, HEAD_DIM), BF16),
            vmem((count, heads * LEVELS), F32),
            vmem((count, heads * LEVELS), BF16),
            vmem((heads, heads * LEVELS, (chunks.bit_length() - 1 + levels_out) * HEAD_DIM), BF16),
            vmem((tokens_out, width), BF16),
            vmem((1, width), F32),
            vmem((tokens_out, width), F32),
            vmem((CHUNK, CHUNK), jnp.int32),
            vmem((heads, count, HEAD_DIM), F32),
            vmem((heads, count, levels_out * HEAD_DIM), BF16),
            vmem((heads, levels_out * HEAD_DIM, HEAD_DIM), BF16),
            vmem((4, heads, HEAD_DIM, HEAD_DIM), BF16),
            vmem((heads, HEAD_DIM, HEAD_DIM), F32),
            vmem((len(PLAN), heads, HEAD_DIM, HEAD_DIM), BF16),
            vmem((heads, chunks - 1, HEAD_DIM, HEAD_DIM), BF16),
            vmem((heads, count, HEAD_DIM), BF16),
            vmem((n_head, heads, tokens_out, HEAD_DIM), BF16),
            vmem((tokens_out, HEAD_DIM), F32),
            dma((heads,)),
            dma((heads,)),
            dma((heads,)),
            dma,
            dma,
            dma,
            dma((sends, heads)),
            dma((sends, heads)),
            pltpu.SemaphoreType.REGULAR((5,)),
            dma((n_head, heads)),
            dma((n_head, heads)),
            dma((heads,)),
        ],
        compiler_params=pltpu.CompilerParams(
            collective_id=0, has_side_effects=True, vmem_limit_bytes=58 << 20
        ),
    )(queries, key_vectors, value_vectors, level_weight, gate_values, norm_gain[None, :])


def solution(mesh):
    placed = (
        P("seq", "head"),
        P("seq", "head"),
        P("seq", "head"),
        P("seq", "head"),
        P(("seq", "head"), None),
        P(),
    )
    return jax.shard_map(
        per_device, mesh=mesh, in_specs=placed, out_specs=P(("seq", "head"), None), check_vma=False
    )
```

time: 61.2 us -> 51.7 us (0.84)
  the two profiles are of different devices: /device:TPU:33 before, /device:TPU:65 now
where the time goes in v2:
time: 51.7 us
  Pallas kernels  50.3 us (97%)
  local copies, waits for them, and re-layouts  1.32 us (3%)
    pallas_call x1, Pallas kernels, per_device(): pl.pallas_call(functools.partial(kernel, n_seq, n_head), out_shape=pltpu....  50.3 us
    unnamed x1, local copies, waits for them, and re-layouts  1.32 us

profile of v2, /device:TPU:65, one launch (start us, length us, event | category | flops | bytes accessed | tf_op | source)
XLA Modules:
  0.0 51.7 jit_solution(17142973365084910591)
XLA Ops:
  0.0 50.3 %shard_map.64 = bf16[128,8192]{1,0:T(8,128)(2,1)S(1)} custom-call(bf16[1024,1024]{1,0:T(8,128)(2,1)} %q_hbm.1, bf16[1024,1024]{1,0:T(8,128)(2,1)} %k_hbm.1, bf16[1024,1024]{1,0:T(8,128)(2,1)} %v_hbm.1, f32[1024,128]{1,0:T(8,128)} %w_hbm.1, bf16[128,8192]{1,0:T(8,128)(2,1)} %gate_hbm.1, f32[1,8192]{1,0:T(1,128)} %bitcast.1), custom_call_target="tpu_custom_call" | custom-call | tf_op jit(solution)/shard_map/pallas_call | solution.py:420
  50.4 1.3 %copy.8 = bf16[128,8192]{1,0:T(8,128)(2,1)} copy(bf16[128,8192]{1,0:T(8,128)(2,1)S(1)} %shard_map.64) | data formatting | bytes 4194304

commit v3 on v2

--- a/solution.py
+++ b/solution.py
@@ -16,7 +16,9 @@
 
 PLAN = ((1, 2, 3), (4, 8, 12), (28, 24))
 PARTS = 2
-DUE = ((1, 2), (6, 3), (11, 4))
+DUE = ((4, 2), (8, 3), (12, 3))
+STATE_DUE = (1, 2)
+ROW0_LATER = 2
 FAR_FIRST = (4, 5, 2, 3, 6, 7, 1)
 
 
@@ -58,7 +60,9 @@
         return tiers.at[h, m * HEAD_DIM : (m + 1) * HEAD_DIM, :]
 
     def landing(s, j, h):
-        return tier_of(2 * s, h) if j == 0 or s == 2 else xbuf.at[2 * s + j - 1, h]
+        if s == 1:
+            return xbuf.at[2 + j, h]
+        return tier_of(2 * s, h) if j == 0 or s == 2 else xbuf.at[j - 1, h]
 
     me_z = lax.shift_right_logical(me_seq, 2)
     in_four = me_z & 3
@@ -190,6 +194,11 @@
                 def _(s=s, j=j):
                     landing(s, j, h)[...] = jnp.zeros((HEAD_DIM, HEAD_DIM), BF16)
 
+        @pl.when(me_z == 0)
+        def _():
+            for m in (2, 3):
+                tier_of(m, h)[...] = jnp.zeros((HEAD_DIM, HEAD_DIM), BF16)
+
     @pl.loop(0, heads)
     def _(h):
         row = lax.broadcasted_iota(jnp.int32, (spread.shape[1], HEAD_DIM), 0)
@@ -218,36 +227,36 @@
         loc[h, loc_slot(first, half)] = left.astype(BF16)
         return left + span_sum(h, first + half, half)
 
-    @pl.loop(0, heads)
-    def _(h):
+    def state(h):
         load_k(h).wait()
         load_v(h).wait()
         total = span_sum(h, 0, chunks)
         run[h] = total
         sbuf[0, h] = total.astype(BF16)
 
-        @pl.when(h == 0)
-        def _():
-            pl.semaphore_wait(
-                barrier, len(plan[0]) + n_head - 1 + in_four + jnp.where(upper, 1, 0)
-            )
-            for j, mask in enumerate(plan[1]):
-                @pl.when((in_four ^ (j + 1)) < in_four)
-                def _(j=j, mask=mask):
-                    pl.semaphore_signal(
-                        ready.at[j], inc=1, device_id=row_partner(mask), device_id_type=MESH
-                    )
-
-            for j, mask in enumerate(plan[2]):
-                @pl.when(receives(2, j))
-                def _(j=j, mask=mask):
-                    pl.semaphore_signal(
-                        ready.at[3 + j], inc=1, device_id=row_partner(mask), device_id_type=MESH
-                    )
-
+    def send_state(h):
         for j in range(len(plan[0])):
             start_exchange(0, j, h)
 
+    state(0)
+    pl.semaphore_wait(
+        barrier, len(plan[0]) + n_head - 1 + in_four + jnp.where(upper, 1, 0)
+    )
+    for j, mask in enumerate(plan[1]):
+        @pl.when((in_four ^ (j + 1)) < in_four)
+        def _(j=j, mask=mask):
+            pl.semaphore_signal(
+                ready.at[j], inc=1, device_id=row_partner(mask), device_id_type=MESH
+            )
+
+    for j, mask in enumerate(plan[2]):
+        @pl.when(receives(2, j))
+        def _(j=j, mask=mask):
+            pl.semaphore_signal(
+                ready.at[3 + j], inc=1, device_id=row_partner(mask), device_id_type=MESH
+            )
+
+    send_state(0)
     load_w.wait()
     slot = lax.broadcasted_iota(jnp.int32, (1, wb.shape[1]), 1) & (LEVELS - 1)
     taken = jnp.ones((1, wb.shape[1]), F32)
@@ -313,14 +322,18 @@
     def service(s, h):
         for j in range(len(plan[s])):
             wait_exchange(s, j, h)
-        pair = None
-        if len(plan[s]) == 3:
-            pair = xbuf[2 * s, h].astype(F32) + xbuf[2 * s + 1, h].astype(F32)
-            tier_of(2 * s + 1, h)[...] = pair.astype(BF16)
         if s < steps - 1:
-            total = run[h] + tier_of(2 * s, h)[...].astype(F32)
-            if pair is not None:
-                total = total + pair
+            nearest = landing(s, 0, h)[...]
+            pair = landing(s, 1, h)[...].astype(F32) + landing(s, 2, h)[...].astype(F32)
+            if s == 0:
+                tier_of(1, h)[...] = pair.astype(BF16)
+            else:
+                @pl.when(me_z != 0)
+                def _():
+                    tier_of(2, h)[...] = nearest
+                    tier_of(3, h)[...] = pair.astype(BF16)
+
+            total = run[h] + nearest.astype(F32) + pair
             run[h] = total
             sbuf[s + 1, h] = total.astype(BF16)
             for j in range(len(plan[s + 1])):
@@ -345,16 +358,30 @@
             scatter(k, h).wait_recv()
         total = sumsq[...]
         for j in range(n_head):
+            at = columns(j * heads + h)
             x = rows[j, h].astype(F32)
             total = total + x * x
+            gsb[:, at] = x * gsb[:, at]
         sumsq[...] = total
 
     units = PARTS * heads
     each = chunks // PARTS
 
-    @pl.loop(0, max(units + heads, DUE[-1][0] + DUE[-1][1] * (heads - 1) + 1))
+    @pl.loop(0, max(units + heads, max(d[0] + d[1] * (heads - 1) for d in DUE) + ROW0_LATER + 1))
     def _(i):
+        later = 1 + (i - STATE_DUE[0]) // STATE_DUE[1]
+
+        @pl.when((i >= STATE_DUE[0]) & (later < heads) & (lax.rem(i - STATE_DUE[0], STATE_DUE[1]) == 0))
+        def _():
+            state(later)
+            send_state(later)
+
         for n, (first, rate) in enumerate(DUE):
+            if n == 1:
+                first = first + jnp.where(me_z == 0, ROW0_LATER, 0)
+            if n == 2:
+                lower_first = jnp.where(me_z == 0, DUE[0][0] + 1, DUE[1][0] + 1)
+                first = jnp.where(upper, first, lower_first)
             h = (i - first) // rate
 
             @pl.when((i >= first) & (h < heads) & (lax.rem(i - first, rate) == 0))
@@ -390,8 +417,7 @@
     def _(j):
         for h in range(heads):
             at = columns(j * heads + h)
-            x = rows[j, h].astype(F32)
-            out_ref[:, at] = (x * sumsq[...] * gsb[:, at]).astype(BF16)
+            out_ref[:, at] = (gsb[:, at] * sumsq[...]).astype(BF16)
 
     @pl.loop(0, heads)
     def _(h):
@@ -436,7 +462,7 @@
             vmem((heads, count, HEAD_DIM), F32),
             vmem((heads, count, levels_out * HEAD_DIM), BF16),
             vmem((heads, levels_out * HEAD_DIM, HEAD_DIM), BF16),
-            vmem((4, heads, HEAD_DIM, HEAD_DIM), BF16),
+            vmem((5, heads, HEAD_DIM, HEAD_DIM), BF16),
             vmem((heads, HEAD_DIM, HEAD_DIM), F32),
             vmem((len(PLAN), heads, HEAD_DIM, HEAD_DIM), BF16),
             vmem((heads, chunks - 1, HEAD_DIM, HEAD_DIM), BF16),

time: 51.7 us -> 47.6 us (0.921)
  the two profiles are of different devices: /device:TPU:65 before, /device:TPU:195 now
where the time goes in v3:
time: 47.6 us; the launch traced here: 47.4 us
  Pallas kernels  46.1 us (97%)
  local copies, waits for them, and re-layouts  1.32 us (3%)
    pallas_call x1, Pallas kernels, per_device(): pl.pallas_call(functools.partial(kernel, n_seq, n_head), out_shape=pltpu....  46.1 us
    unnamed x1, local copies, waits for them, and re-layouts  1.32 us

profile of v3, /device:TPU:195, one launch (start us, length us, event | category | flops | bytes accessed | tf_op | source)
XLA Modules:
  0.0 47.4 jit_solution(9597368575799104446)
XLA Ops:
  0.0 46.1 %shard_map.64 = bf16[128,8192]{1,0:T(8,128)(2,1)S(1)} custom-call(bf16[1024,1024]{1,0:T(8,128)(2,1)} %q_hbm.1, bf16[1024,1024]{1,0:T(8,128)(2,1)} %k_hbm.1, bf16[1024,1024]{1,0:T(8,128)(2,1)} %v_hbm.1, f32[1024,128]{1,0:T(8,128)} %w_hbm.1, bf16[128,8192]{1,0:T(8,128)(2,1)} %gate_hbm.1, f32[1,8192]{1,0:T(1,128)} %bitcast.1), custom_call_target="tpu_custom_call" | custom-call | tf_op jit(solution)/shard_map/pallas_call | solution.py:446
  46.1 1.3 %copy.8 = bf16[128,8192]{1,0:T(8,128)(2,1)} copy(bf16[128,8192]{1,0:T(8,128)(2,1)S(1)} %shard_map.64) | data formatting | bytes 4194304

commit v4 on v3

--- a/solution.py
+++ b/solution.py
@@ -24,9 +24,9 @@
 
 def kernel(
     n_seq, n_head, q_hbm, k_hbm, v_hbm, w_hbm, gate_hbm, gain_hbm, out_ref,
-    qb, kb, vb, wb, wlow, spread, gateb, gainb, gsb, levb, inner, wq, tiers, xbuf, run, sbuf, loc, att, rows, sumsq,
-    q_sem, k_sem, v_sem, w_sem, gate_sem, gain_sem,
-    xs_sem, xr_sem, ready, ys_sem, yr_sem, keep_sem,
+    qb, kvb, wb, wlow, spread, gateb, gainb, gsb, levb, inner, wq, tiers, xbuf, run, sbuf, loc, att, rows, sumsq,
+    q_sem, kv_sem, w_sem, gate_sem, gain_sem,
+    xs_sem, xr_sem, ready, ys_sem, yr_sem,
 ):
     plan = PLAN
     steps = len(plan)
@@ -44,13 +44,16 @@
         return pl.ds(pl.multiple_of(h * HEAD_DIM, HEAD_DIM), HEAD_DIM)
 
     def load_k(h):
-        return pltpu.make_async_copy(k_hbm.at[:, columns(h)], kb.at[h], k_sem.at[h])
+        return pltpu.make_async_copy(k_hbm.at[:, columns(h)], kvb.at[h, 0], kv_sem.at[jnp.minimum(h, 1)])
 
     def load_v(h):
-        return pltpu.make_async_copy(v_hbm.at[:, columns(h)], vb.at[h], v_sem.at[h])
+        return pltpu.make_async_copy(v_hbm.at[:, columns(h)], kvb.at[h, 1], kv_sem.at[jnp.minimum(h, 1)])
 
     def load_q(h):
-        return pltpu.make_async_copy(q_hbm.at[:, columns(h)], qb.at[h], q_sem.at[h])
+        return pltpu.make_async_copy(q_hbm.at[:, columns(h)], qb.at[h], q_sem)
+
+    def wait_for(ref, sem):
+        pltpu.make_async_copy(ref, ref, sem).wait()
 
     load_w = pltpu.make_async_copy(w_hbm, wb, w_sem)
     load_gate = pltpu.make_async_copy(gate_hbm, gateb, gate_sem)
@@ -102,14 +105,21 @@
                     pl.semaphore_wait(ready.at[3 + j], 1)
             exchange(s, j, h).start()
 
-    def wait_exchange(s, j, h):
+    def wait_exchange(s, h):
+        def wait(pieces):
+            wait_for(sbuf.at[0, 0:pieces], xr_sem.at[s, h])
+
         if s == 0:
-            exchange(s, j, h).wait_recv()
-            return
-
-        @pl.when(receives(s, j))
-        def _():
-            exchange(s, j, h).wait_recv()
+            wait(3)
+        elif s == 1:
+            for pieces in (1, 2, 3):
+                @pl.when((in_four == pieces) | ((me_z == 0) & (pieces == 3)))
+                def _(pieces=pieces):
+                    wait(pieces)
+        else:
+            @pl.when(upper)
+            def _():
+                wait(1)
 
     def row_partner(mask):
         return {"seq": me_seq ^ mask}
@@ -119,8 +129,8 @@
         return pltpu.make_async_remote_copy(
             src_ref=sbuf.at[s, h],
             dst_ref=landing(s, j, h),
-            send_sem=xs_sem.at[n, h],
-            recv_sem=xr_sem.at[n, h],
+            send_sem=xs_sem.at[n],
+            recv_sem=xr_sem.at[s, h],
             device_id={"seq": me_seq ^ plan[s][j]},
             device_id_type=MESH,
         )
@@ -132,14 +142,14 @@
         return pltpu.make_async_remote_copy(
             src_ref=att.at[h, tokens_of(me_head ^ k), :],
             dst_ref=rows.at[me_head, h],
-            send_sem=ys_sem.at[k, h],
-            recv_sem=yr_sem.at[k, h],
+            send_sem=ys_sem,
+            recv_sem=yr_sem.at[h],
             device_id={"head": me_head ^ k},
             device_id_type=MESH,
         )
 
     def keep(h):
-        return pltpu.make_async_copy(att.at[h, tokens_of(me_head), :], rows.at[me_head, h], keep_sem.at[h])
+        return pltpu.make_async_copy(att.at[h, tokens_of(me_head), :], rows.at[me_head, h], yr_sem.at[h])
 
     load_k(0).start()
     load_v(0).start()
@@ -209,7 +219,7 @@
     def part(h, c):
         at = slice(c * CHUNK, (c + 1) * CHUNK)
         return lax.dot_general(
-            kb[h, at, :], vb[h, at, :], (((0,), (0,)), ((), ())), preferred_element_type=F32
+            kvb[h, 0, at, :], kvb[h, 1, at, :], (((0,), (0,)), ((), ())), preferred_element_type=F32
         )
 
     def loc_slot(first, half):
@@ -228,8 +238,6 @@
         return left + span_sum(h, first + half, half)
 
     def state(h):
-        load_k(h).wait()
-        load_v(h).wait()
         total = span_sum(h, 0, chunks)
         run[h] = total
         sbuf[0, h] = total.astype(BF16)
@@ -238,6 +246,7 @@
         for j in range(len(plan[0])):
             start_exchange(0, j, h)
 
+    wait_for(kvb.at[0], kv_sem.at[0])
     state(0)
     pl.semaphore_wait(
         barrier, len(plan[0]) + n_head - 1 + in_four + jnp.where(upper, 1, 0)
@@ -289,7 +298,7 @@
             at = slice(c * CHUNK, (c + 1) * CHUNK)
             scores.append(
                 lax.dot_general(
-                    qb[h, at, :], kb[h, at, :], (((1,), (1,)), ((), ())), preferred_element_type=F32
+                    qb[h, at, :], kvb[h, 0, at, :], (((1,), (1,)), ((), ())), preferred_element_type=F32
                 )
             )
         for n in range(0, levels_out, 2):
@@ -310,7 +319,7 @@
             lefts.append((c, bits, left))
         for c, bits, left in lefts:
             at = slice(c * CHUNK, (c + 1) * CHUNK)
-            right = [vb[h, at, :]] + [
+            right = [kvb[h, 1, at, :]] + [
                 loc[h, loc_slot((c >> n << n) - (1 << n), 1 << n)] for n in bits
             ]
             inner[h, at, :] = jnp.dot(
@@ -320,8 +329,7 @@
             )
 
     def service(s, h):
-        for j in range(len(plan[s])):
-            wait_exchange(s, j, h)
+        wait_exchange(s, h)
         if s < steps - 1:
             nearest = landing(s, 0, h)[...]
             pair = landing(s, 1, h)[...].astype(F32) + landing(s, 2, h)[...].astype(F32)
@@ -352,10 +360,21 @@
         gate = gateb[:, at].astype(F32)
         gsb[:, at] = gainb[:, at] * (gate / (1.0 + jnp.exp(-gate)))
 
+    def exchanged():
+        n = 0
+        for s in range(steps):
+            for j in range(len(plan[s])):
+                if s == 0:
+                    wait_for(sbuf.at[s], xs_sem.at[n])
+                else:
+                    @pl.when(sends(s, j))
+                    def _(s=s, n=n):
+                        wait_for(sbuf.at[s], xs_sem.at[n])
+
+                n += 1
+
     def collect(h):
-        keep(h).wait()
-        for k in range(1, n_head):
-            scatter(k, h).wait_recv()
+        wait_for(rows.at[0], yr_sem.at[h])
         total = sumsq[...]
         for j in range(n_head):
             at = columns(j * heads + h)
@@ -373,6 +392,10 @@
 
         @pl.when((i >= STATE_DUE[0]) & (later < heads) & (lax.rem(i - STATE_DUE[0], STATE_DUE[1]) == 0))
         def _():
+            @pl.when(later == 1)
+            def _():
+                wait_for(kvb.at[1:heads], kv_sem.at[1])
+
             state(later)
             send_state(later)
 
@@ -393,7 +416,10 @@
             def _(p=p):
                 h = i // PARTS
                 if p == 0:
-                    load_q(h).wait()
+                    @pl.when(i == 0)
+                    def _():
+                        wait_for(qb, q_sem)
+
                 inside(h, range(p * each, (p + 1) * each))
 
         @pl.when(i == units)
@@ -404,6 +430,8 @@
         @pl.when((i >= units) & (i < units + heads))
         def _():
             gating(i - units)
+
+    exchanged()
 
     @pl.loop(0, heads)
     def _(h):
@@ -419,19 +447,7 @@
             at = columns(j * heads + h)
             out_ref[:, at] = (gsb[:, at] * sumsq[...]).astype(BF16)
 
-    @pl.loop(0, heads)
-    def _(h):
-        for s in range(steps):
-            for j in range(len(plan[s])):
-                if s == 0:
-                    exchange(s, j, h).wait_send()
-                else:
-                    @pl.when(sends(s, j))
-                    def _(s=s, j=j):
-                        exchange(s, j, h).wait_send()
-
-        for k in range(1, n_head):
-            scatter(k, h).wait_send()
+    wait_for(att.at[0 : heads * (n_head - 1) // n_head], ys_sem)
 
 
 def per_device(queries, key_vectors, value_vectors, level_weight, gate_values, norm_gain):
@@ -450,8 +466,7 @@
         out_specs=pl.BlockSpec(memory_space=pltpu.VMEM),
         scratch_shapes=[
             vmem((heads, count, HEAD_DIM), BF16),
-            vmem((heads, count, HEAD_DIM), BF16),
-            vmem((heads, count, HEAD_DIM), BF16),
+            vmem((heads, 2, count, HEAD_DIM), BF16),
             vmem((count, heads * LEVELS), F32),
             vmem((count, heads * LEVELS), BF16),
             vmem((heads, heads * LEVELS, (chunks.bit_length() - 1 + levels_out) * HEAD_DIM), BF16),
@@ -469,17 +484,15 @@
             vmem((heads, count, HEAD_DIM), BF16),
             vmem((n_head, heads, tokens_out, HEAD_DIM), BF16),
             vmem((tokens_out, HEAD_DIM), F32),
-            dma((heads,)),
-            dma((heads,)),
-            dma((heads,)),
+            dma,
+            dma((2,)),
             dma,
             dma,
             dma,
-            dma((sends, heads)),
-            dma((sends, heads)),
+            dma((sends,)),
+            dma((len(PLAN), heads)),
             pltpu.SemaphoreType.REGULAR((5,)),
-            dma((n_head, heads)),
-            dma((n_head, heads)),
+            dma,
             dma((heads,)),
         ],
         compiler_params=pltpu.CompilerParams(

time: 47.6 us -> 45.6 us (0.958)
  Pallas kernels: 46.1 us -> 44.2 us
    pallas_call x1, Pallas kernels: 46.1 us -> 44.2 us  [per_device(): pl.pallas_call(functools.partial(kernel, n_seq, n_head), out_shape=pltpu....]
where the time goes in v4:
time: 45.6 us; the launch traced here: 45.5 us
  Pallas kernels  44.2 us (97%)
  local copies, waits for them, and re-layouts  1.32 us (3%)
    pallas_call x1, Pallas kernels, per_device(): pl.pallas_call(functools.partial(kernel, n_seq, n_head), out_shape=pltpu....  44.2 us
    unnamed x1, local copies, waits for them, and re-layouts  1.32 us

profile of v4, /device:TPU:195, one launch (start us, length us, event | category | flops | bytes accessed | tf_op | source)
XLA Modules:
  0.0 45.5 jit_solution(15318790428313136968)
XLA Ops:
  0.0 44.2 %shard_map.64 = bf16[128,8192]{1,0:T(8,128)(2,1)S(1)} custom-call(bf16[1024,1024]{1,0:T(8,128)(2,1)} %q_hbm.1, bf16[1024,1024]{1,0:T(8,128)(2,1)} %k_hbm.1, bf16[1024,1024]{1,0:T(8,128)(2,1)} %v_hbm.1, f32[1024,128]{1,0:T(8,128)} %w_hbm.1, bf16[128,8192]{1,0:T(8,128)(2,1)} %gate_hbm.1, f32[1,8192]{1,0:T(1,128)} %bitcast.1), custom_call_target="tpu_custom_call" | custom-call | tf_op jit(solution)/shard_map/pallas_call | solution.py:462
  44.2 1.3 %copy.8 = bf16[128,8192]{1,0:T(8,128)(2,1)} copy(bf16[128,8192]{1,0:T(8,128)(2,1)S(1)} %shard_map.64) | data formatting | bytes 4194304

commit v5 on v4

--- a/solution.py
+++ b/solution.py
@@ -16,9 +16,9 @@
 
 PLAN = ((1, 2, 3), (4, 8, 12), (28, 24))
 PARTS = 2
-DUE = ((4, 2), (8, 3), (12, 3))
+DUE = ((4, 2), (8, 3), (11, 3))
 STATE_DUE = (1, 2)
-ROW0_LATER = 2
+ROW0_LATER = 0
 FAR_FIRST = (4, 5, 2, 3, 6, 7, 1)
 
 
@@ -438,15 +438,10 @@
         collect(h)
 
     mean_square = jnp.sum(sumsq[...], axis=1, keepdims=True) * (1.0 / (heads * n_head * HEAD_DIM))
-    scale = jnp.broadcast_to(lax.rsqrt(mean_square + 1e-06), (tokens_out, HEAD_DIM))
-    sumsq[...] = scale
-
-    @pl.loop(0, n_head)
-    def _(j):
-        for h in range(heads):
-            at = columns(j * heads + h)
-            out_ref[:, at] = (gsb[:, at] * sumsq[...]).astype(BF16)
-
+    scale = lax.rsqrt(mean_square + 1e-06)
+    tile = 16
+    for r in range(0, tokens_out, tile):
+        out_ref[r : r + tile, :] = (gsb[r : r + tile, :] * scale[r : r + tile, :]).astype(BF16)
     wait_for(att.at[0 : heads * (n_head - 1) // n_head], ys_sem)
 
 

time: 45.6 us -> 44.2 us (0.969)
  Pallas kernels: 44.2 us -> 42.8 us
    pallas_call x1, Pallas kernels: 44.2 us -> 42.8 us  [per_device(): pl.pallas_call(functools.partial(kernel, n_seq, n_head), out_shape=pltpu....]
where the time goes in v5:
time: 44.2 us; the launch traced here: 44.1 us
  Pallas kernels  42.8 us (97%)
  local copies, waits for them, and re-layouts  1.32 us (3%)
    pallas_call x1, Pallas kernels, per_device(): pl.pallas_call(functools.partial(kernel, n_seq, n_head), out_shape=pltpu....  42.8 us
    unnamed x1, local copies, waits for them, and re-layouts  1.32 us

profile of v5, /device:TPU:195, one launch (start us, length us, event | category | flops | bytes accessed | tf_op | source)
XLA Modules:
  0.0 44.1 jit_solution(12825633624260509116)
XLA Ops:
  0.0 42.8 %shard_map.64 = bf16[128,8192]{1,0:T(8,128)(2,1)S(1)} custom-call(bf16[1024,1024]{1,0:T(8,128)(2,1)} %q_hbm.1, bf16[1024,1024]{1,0:T(8,128)(2,1)} %k_hbm.1, bf16[1024,1024]{1,0:T(8,128)(2,1)} %v_hbm.1, f32[1024,128]{1,0:T(8,128)} %w_hbm.1, bf16[128,8192]{1,0:T(8,128)(2,1)} %gate_hbm.1, f32[1,8192]{1,0:T(1,128)} %bitcast.1), custom_call_target="tpu_custom_call" | custom-call | tf_op jit(solution)/shard_map/pallas_call | solution.py:457
  42.8 1.3 %copy.8 = bf16[128,8192]{1,0:T(8,128)(2,1)} copy(bf16[128,8192]{1,0:T(8,128)(2,1)S(1)} %shard_map.64) | data formatting | bytes 4194304

commit v6 on v5

--- a/solution.py
+++ b/solution.py
@@ -399,7 +399,8 @@
             state(later)
             send_state(later)
 
-        for n, (first, rate) in enumerate(DUE):
+        for n in (0, 2, 1):
+            first, rate = DUE[n]
             if n == 1:
                 first = first + jnp.where(me_z == 0, ROW0_LATER, 0)
             if n == 2:

time: 44.2 us -> 43.4 us (0.982)
  Pallas kernels: 42.8 us -> 41.9 us
    pallas_call x1, Pallas kernels: 42.8 us -> 41.9 us  [per_device(): pl.pallas_call(functools.partial(kernel, n_seq, n_head), out_shape=pltpu....]
where the time goes in v6:
time: 43.4 us; the launch traced here: 43.2 us
  Pallas kernels  41.9 us (97%)
  local copies, waits for them, and re-layouts  1.32 us (3%)
    pallas_call x1, Pallas kernels, per_device(): pl.pallas_call(functools.partial(kernel, n_seq, n_head), out_shape=pltpu....  41.9 us
    unnamed x1, local copies, waits for them, and re-layouts  1.32 us

profile of v6, /device:TPU:195, one launch (start us, length us, event | category | flops | bytes accessed | tf_op | source)
XLA Modules:
  0.0 43.2 jit_solution(8932807101775127737)
XLA Ops:
  0.0 41.9 %shard_map.64 = bf16[128,8192]{1,0:T(8,128)(2,1)S(1)} custom-call(bf16[1024,1024]{1,0:T(8,128)(2,1)} %q_hbm.1, bf16[1024,1024]{1,0:T(8,128)(2,1)} %k_hbm.1, bf16[1024,1024]{1,0:T(8,128)(2,1)} %v_hbm.1, f32[1024,128]{1,0:T(8,128)} %w_hbm.1, bf16[128,8192]{1,0:T(8,128)(2,1)} %gate_hbm.1, f32[1,8192]{1,0:T(1,128)} %bitcast.1), custom_call_target="tpu_custom_call" | custom-call | tf_op jit(solution)/shard_map/pallas_call | solution.py:458
  41.9 1.3 %copy.8 = bf16[128,8192]{1,0:T(8,128)(2,1)} copy(bf16[128,8192]{1,0:T(8,128)(2,1)S(1)} %shard_map.64) | data formatting | bytes 4194304
